TPU v7x, 32 devices: a whole 2x2x4 slice. The times are simulated.
32 devices in a mesh: dp: 16 (over z, y, x), tensor: 2 (over core).
Axes of the slice: x: 2, y: 2, z: 4, core: 2. Of those that a mesh axis runs over, the one named last changes fastest.
Arguments:
- grads: bfloat16 [16, 256, 3584], P('dp', None, 'tensor'), may hold values from -6 to 6
- residual: float32 [16, 256, 3584], P('dp', None, 'tensor'), may hold values from -4 to 4
- q_prev: float32 [3584, 64], P('tensor'), may hold values from -6 to 6
Outputs:
- q_next: float32 [3584, 64], P('tensor')
- basis: float32 [256, 64], replicated
- new_residual: float32 [16, 256, 3584], P('dp', None, 'tensor')
All inputs are finite; a program needn't handle non-finite values.
Results may differ from a plain program's by a relative error of at most 0.0003.
Values sent between devices are 32-bit elements; how exact they have to be, the bound alone decides.
A program may use at most 64 MiB of HBM per device.

v0:
```python
import jax
import jax.numpy as jnp
from jax import lax
from jax.sharding import PartitionSpec as P


def local(grads, residual, q_prev):
    high = lax.Precision.HIGHEST
    count = lax.axis_size("dp")
    merged = grads[0].astype(jnp.float32) + residual[0]
    partial_left = jnp.dot(merged, q_prev, precision=high)
    left = lax.psum(partial_left, ("dp", "tensor")) / count
    gram = jnp.dot(left.T, left, precision=high)
    lower = jnp.linalg.cholesky(gram)
    basis = jax.scipy.linalg.solve_triangular(lower, left.T, lower=True).T
    q_next = lax.psum(jnp.dot(merged.T, basis, precision=high), "dp") / count
    update = jnp.dot(basis, q_next.T, precision=high)
    new_residual = merged - update
    return (q_next, basis, new_residual[None])


def solution(mesh):
    in_specs = (P("dp", None, "tensor"), P("dp", None, "tensor"), P("tensor", None))
    out_specs = (P("tensor", None), P(), P("dp", None, "tensor"))
    return jax.shard_map(local, mesh=mesh, in_specs=in_specs, out_specs=out_specs, check_vma=False)
```

profile of v0, /device:TPU:0, one launch (start us, length us, event | category | flops | bytes accessed | tf_op | source)
XLA Modules:
  0.0 274.1 jit_solution(10268975559233325000)
XLA Ops:
  7.2 0.0 copy-start
  7.2 0.0 copy-start.1
  7.2 0.0 copy-start.2
  7.2 0.0 all-reduce.3.cloned.1.call-start
  7.2 0.9 copy-done
  8.2 4.2 %fusion.3 = f32[256,64]{0,1:T(8,128)} fusion(f32[1792,64]{0,1:T(8,128)S(1)} %copy-done, f32[1,256,1792]{2,1,0:T(8,128)} %param.4, bf16[1,256,1792]{2,1,0:T(8,128)(2,1)} %param.3), kind=kOutput, calls=%fused_computation.4 | convolution fusion | flops 353239040 | bytes 3276800 | tf_op jit(solution)/shard_map/dot_general | solution.py:11
  12.4 0.0 all-reduce.3.cloned.1.call-update
  12.4 0.0 all-reduce.5.cloned.1.call-start
  12.4 123.9 %all-reduce.3.cloned.1.call-done = f32[256,64]{0,1:T(8,128)} async-done(((f32[256,64]{0,1:T(8,128)}), f32[256,64]{0,1:T(8,128)}) %all-reduce.3.cloned.1.call-update) | async-done | bytes 65552 | tf_op jit(solution)/shard_map/psum | solution.py:12
  136.3 1.1 fusion.7
  137.4 0.1 copy.6
  137.5 5.8 %cholesky.16 = f32[64,64]{1,0:T(8,128)S(1)} custom-call(f32[64,64]{1,0:T(8,128)S(1)} %fusion.11), custom_call_target="Cholesky" | custom-call | tf_op jit(solution)/shard_map/jit(cholesky)/cholesky | solution.py:14
  143.4 0.6 compare_reduce_fusion
  144.0 0.7 fusion.9
  144.7 4.9 %custom-call.7 = f32[1,64,64]{1,2,0:T(8,128)S(1)} custom-call(f32[1,64,64]{2,1,0:T(8,128)S(1)} %fusion.9), custom_call_target="InvertDiagBlocksLowerTriangular" | custom-call | tf_op jit(solution)/shard_map/jit(_solve_triangular)/triangular_solve | solution.py:15
  149.6 1.1 fusion.5
  150.7 0.0 copy-done.1
  150.7 0.0 copy-done.2
  150.7 0.0 copy-start.4
  150.7 2.2 fusion.1
  152.9 0.0 all-reduce.5.cloned.1.call-update
  152.9 110.3 %all-reduce.5.cloned.1.call-done = f32[1792,64]{0,1:T(8,128)} async-done(((f32[1792,64]{0,1:T(8,128)}), f32[1792,64]{0,1:T(8,128)}) %all-reduce.5.cloned.1.call-update) | async-done | bytes 458768 | tf_op jit(solution)/shard_map/psum | solution.py:16
  263.3 1.0 broadcast_multiply_fusion
  264.3 0.0 copy-done.4
  264.3 0.0 copy-start.3
  264.3 2.9 %fusion = f32[1,256,1792]{2,1,0:T(8,128)} fusion(f32[64,256]{1,0:T(8,128)S(1)} %fusion.5, f32[1792,64]{0,1:T(8,128)S(1)} %broadcast_multiply_fusion, f32[1,256,1792]{2,1,0:T(8,128)S(1)} %copy-done.1, bf16[1,256,1792]{2,1,0:T(8,128)(2,1)S(1)} %copy-done.2), kind=kOutput, calls=%fused_computation.1 | convolution fusion | flops 353697792 | bytes 5111808 | tf_op jit(solution)/shard_map/dot_general | solution.py:17
  267.2 0.0 copy-done.3
  (2 shorter events, 0.0 us)
Async XLA Ops:
  7.2 1.0 copy-start
  7.2 143.5 %copy-start.1 = (f32[1,256,1792]{2,1,0:T(8,128)S(1)}, f32[1,256,1792]{2,1,0:T(8,128)}, u32[]{:S(2)}) copy-start(f32[1,256,1792]{2,1,0:T(8,128)} %param.4) | copy-start | bytes 5505028
  7.2 143.5 %copy-start.2 = (bf16[1,256,1792]{2,1,0:T(8,128)(2,1)S(1)}, bf16[1,256,1792]{2,1,0:T(8,128)(2,1)}, u32[]{:S(2)}) copy-start(bf16[1,256,1792]{2,1,0:T(8,128)(2,1)} %param.3) | copy-start | bytes 2752516
  7.2 129.1 %all-reduce.3.cloned.1.call-start = ((), (), s32[]{:S(2)}) async-start(), calls=%async_computation | async-start | bytes 131072 | tf_op jit(solution)/shard_map/psum | solution.py:12
  12.4 250.9 %all-reduce.5.cloned.1.call-start = ((), (), s32[]{:S(2)}) async-start(), calls=%async_computation.1 | async-start | bytes 917504 | tf_op jit(solution)/shard_map/psum | solution.py:16
  150.7 113.6 %copy-start.4 = (f32[64,256]{1,0:T(8,128)}, f32[64,256]{1,0:T(8,128)S(1)}, u32[]{:S(2)}) copy-start(f32[64,256]{1,0:T(8,128)S(1)} %fusion.5) | copy-start | bytes 196612
  264.3 2.9 %copy-start.3 = (f32[1792,64]{0,1:T(8,128)}, f32[1792,64]{0,1:T(8,128)S(1)}, u32[]{:S(2)}) copy-start(f32[1792,64]{0,1:T(8,128)S(1)} %broadcast_multiply_fusion) | copy-start | bytes 1376260
Sparse Core Ops, SparseCore 0:
  14.2 122.1 all-reduce.2
  153.1 110.1 all-reduce.4
where the time goes:
time: 274 us
  waiting for transfers between devices  234 us (85%)
  between operations  14.1 us (5%)
  other arithmetic  13.1 us (5%)
  matrix products  11.4 us (4%)
    psum x1, waiting for transfers between devices, local(): left = lax.psum(partial_left, ('dp', 'tensor')) / count  124 us
    psum x1, waiting for transfers between devices, local(): q_next = lax.psum(jnp.dot(merged.T, basis, precision=high), 'dp') / count  110 us
    another operation x3, other arithmetic, local(): lower = jnp.linalg.cholesky(gram)  6.52 us
    another operation x2, other arithmetic, local(): basis = jax.scipy.linalg.solve_triangular(lower, left.T, lower=True).T  5.55 us
  transfers between devices with their start and end apart: 2, of which 2 were waited for; matrix products, arithmetic and copies ran while one was open for 0% of the time, Pallas kernels for 0%

commit v1 on v0

--- a/solution.py
+++ b/solution.py
@@ -1,7 +1,15 @@
+import functools
 import jax
 import jax.numpy as jnp
 from jax import lax
 from jax.sharding import PartitionSpec as P
+
+
+def pass_the_orders(z_in, axis_id):
+    return lax.all_gather(z_in, axis_id).sum(axis=0)
+
+
+bind_the_targets = functools.partial(pass_the_orders, axis_id=("dp", "tensor"))
 
 
 def local(grads, residual, q_prev):
@@ -9,7 +17,7 @@
     count = lax.axis_size("dp")
     merged = grads[0].astype(jnp.float32) + residual[0]
     partial_left = jnp.dot(merged, q_prev, precision=high)
-    left = lax.psum(partial_left, ("dp", "tensor")) / count
+    left = bind_the_targets(partial_left) / count
     gram = jnp.dot(left.T, left, precision=high)
     lower = jnp.linalg.cholesky(gram)
     basis = jax.scipy.linalg.solve_triangular(lower, left.T, lower=True).T

time: 274 us -> 207 us (0.76)
  waiting for transfers between devices: 234 us -> 166 us
    psum x1 -> x0, waiting for transfers between devices: 124 us -> none  [local(): left = lax.psum(partial_left, ('dp', 'tensor')) / count]
    all_gather x0 -> x1, waiting for transfers between devices: none -> 57.6 us  [pass_the_orders(): return lax.all_gather(z_in, axis_id).sum(axis=0)]
where the time goes in v1:
time: 207 us
  waiting for transfers between devices  166 us (80%)
  between operations  14.1 us (7%)
  other arithmetic  13.3 us (6%)
  matrix products  9.69 us (5%)
  local copies, waits for them, and re-layouts  3.37 us (2%)
    psum x1, waiting for transfers between devices, local(): q_next = lax.psum(jnp.dot(merged.T, basis, precision=high), 'dp') / count  108 us
    all_gather x1, waiting for transfers between devices, pass_the_orders(): return lax.all_gather(z_in, axis_id).sum(axis=0)  57.6 us
    another operation x3, other arithmetic, local(): lower = jnp.linalg.cholesky(gram)  6.52 us
    another operation x2, other arithmetic, local(): basis = jax.scipy.linalg.solve_triangular(lower, left.T, lower=True).T  5.55 us
    dot_general x1, matrix products, local(): partial_left = jnp.dot(merged, q_prev, precision=high)  4.17 us
  transfers between devices with their start and end apart: 2, of which 2 were waited for; matrix products, arithmetic and copies ran while one was open for 0% of the time, Pallas kernels for 0%

profile of v1, /device:TPU:0, one launch (start us, length us, event | category | flops | bytes accessed | tf_op | source)
XLA Modules:
  0.0 206.8 jit_solution(14840862912151061973)
XLA Ops:
  7.2 0.0 copy-start
  7.2 0.0 all-gather.3.cloned.1.call-start
  7.2 1.0 copy-done
  8.2 4.2 %fusion.3 = f32[256,64]{0,1:T(8,128)} fusion(f32[1792,64]{0,1:T(8,128)S(1)} %copy-done, f32[1,256,1792]{2,1,0:T(8,128)} %param.4, bf16[1,256,1792]{2,1,0:T(8,128)(2,1)} %param.3), kind=kOutput, calls=%fused_computation.5 | convolution fusion | flops 353239040 | bytes 3276800 | tf_op jit(solution)/shard_map/dot_general | solution.py:19
  12.4 0.0 all-gather.3.cloned.1.call-update
  12.4 0.0 all-reduce.2.cloned.1.call-start
  12.4 57.6 %all-gather.3.cloned.1.call-done = f32[8192,64]{0,1:T(8,128)} async-done(((f32[256,64]{0,1:T(8,128)}), f32[8192,64]{0,1:T(8,128)}) %all-gather.3.cloned.1.call-update) | async-done | bytes 2097168 | tf_op jit(solution)/shard_map/all_gather | solution.py:9
  70.1 0.0 copy-start.2
  70.1 2.3 %copy.8 = f32[8,8,32,256]{3,2,1,0:T(8,128)S(1)} copy(f32[8,8,32,256]{3,1,2,0:T(8,128)} %bitcast.27) | data formatting | bytes 4194304
  72.4 0.0 copy-start.1
  72.4 0.2 bitcast_reduce_fusion
  72.6 0.2 fusion.7
  72.8 0.1 copy.7
  72.9 5.8 %cholesky.16 = f32[64,64]{1,0:T(8,128)S(1)} custom-call(f32[64,64]{1,0:T(8,128)S(1)} %fusion.11), custom_call_target="Cholesky" | custom-call | tf_op jit(solution)/shard_map/jit(cholesky)/cholesky | solution.py:22
  78.8 0.6 compare_reduce_fusion
  79.5 0.7 fusion.9
  80.1 4.9 %custom-call.7 = f32[1,64,64]{1,2,0:T(8,128)S(1)} custom-call(f32[1,64,64]{2,1,0:T(8,128)S(1)} %fusion.9), custom_call_target="InvertDiagBlocksLowerTriangular" | custom-call | tf_op jit(solution)/shard_map/jit(_solve_triangular)/triangular_solve | solution.py:23
  85.0 0.3 fusion.5
  85.3 0.0 copy-done.2
  85.3 0.0 copy-done.1
  85.3 0.0 copy-start.4
  85.3 2.2 %fusion.1 = f32[1792,64]{0,1:T(8,128)} fusion(f32[64,256]{1,0:T(8,128)S(1)} %fusion.5, f32[1,256,1792]{2,1,0:T(8,128)S(1)} %copy-done.1, bf16[1,256,1792]{2,1,0:T(8,128)(2,1)S(1)} %copy-done.2), kind=kOutput, calls=%fused_computation.3 | convolution fusion | flops 353239040 | bytes 3276800 | tf_op jit(solution)/shard_map/dot_general | solution.py:24
  87.5 0.0 all-reduce.2.cloned.1.call-update
  87.5 108.5 %all-reduce.2.cloned.1.call-done = f32[1792,64]{0,1:T(8,128)} async-done(((f32[1792,64]{0,1:T(8,128)}), f32[1792,64]{0,1:T(8,128)}) %all-reduce.2.cloned.1.call-update) | async-done | bytes 458768 | tf_op jit(solution)/shard_map/psum | solution.py:24
  196.0 1.0 broadcast_multiply_fusion
  197.0 0.0 copy-done.4
  197.1 0.0 copy-start.3
  197.1 2.9 %fusion = f32[1,256,1792]{2,1,0:T(8,128)} fusion(f32[64,256]{1,0:T(8,128)S(1)} %fusion.5, f32[1792,64]{0,1:T(8,128)S(1)} %broadcast_multiply_fusion, f32[1,256,1792]{2,1,0:T(8,128)S(1)} %copy-done.1, bf16[1,256,1792]{2,1,0:T(8,128)(2,1)S(1)} %copy-done.2), kind=kOutput, calls=%fused_computation.1 | convolution fusion | flops 353697792 | bytes 5111808 | tf_op jit(solution)/shard_map/dot_general | solution.py:25
  200.0 0.0 copy-done.3
  (2 shorter events, 0.0 us)
Async XLA Ops:
  7.2 1.0 copy-start
  7.2 62.9 %all-gather.3.cloned.1.call-start = ((), (), s32[]{:S(2)}) async-start(), calls=%async_computation.1 | async-start | bytes 2162688 | tf_op jit(solution)/shard_map/all_gather | solution.py:9
  12.4 183.6 %all-reduce.2.cloned.1.call-start = ((), (), s32[]{:S(2)}) async-start(), calls=%async_computation | async-start | bytes 917504 | tf_op jit(solution)/shard_map/psum | solution.py:24
  70.1 15.2 %copy-start.2 = (bf16[1,256,1792]{2,1,0:T(8,128)(2,1)S(1)}, bf16[1,256,1792]{2,1,0:T(8,128)(2,1)}, u32[]{:S(2)}) copy-start(bf16[1,256,1792]{2,1,0:T(8,128)(2,1)} %param.3) | copy-start | bytes 2752516
  72.4 12.9 %copy-start.1 = (f32[1,256,1792]{2,1,0:T(8,128)S(1)}, f32[1,256,1792]{2,1,0:T(8,128)}, u32[]{:S(2)}) copy-start(f32[1,256,1792]{2,1,0:T(8,128)} %param.4) | copy-start | bytes 5505028
  85.3 111.7 %copy-start.4 = (f32[64,256]{1,0:T(8,128)}, f32[64,256]{1,0:T(8,128)S(1)}, u32[]{:S(2)}) copy-start(f32[64,256]{1,0:T(8,128)S(1)} %fusion.5) | copy-start | bytes 196612
  197.1 2.9 %copy-start.3 = (f32[1792,64]{0,1:T(8,128)}, f32[1792,64]{0,1:T(8,128)S(1)}, u32[]{:S(2)}) copy-start(f32[1792,64]{0,1:T(8,128)S(1)} %broadcast_multiply_fusion) | copy-start | bytes 1376260
Sparse Core Ops, SparseCore 0:
  12.5 57.5 all-gather.2
  87.6 108.3 all-reduce.1
